TPU v7x, 32 devices: a whole 2x2x4 slice. The times are simulated.
32 devices in a mesh: band: 2 (over core), grid: 16 (over z, y, x).
Axes of the slice: x: 2, y: 2, z: 4, core: 2. Of those that a mesh axis runs over, the one named last changes fastest.
Arguments:
- coefficients: float32 [4, 2, 128, 128, 128], P('band', None, 'grid'), may hold values from -0.01171875 to 0.01171875
- potential: float32 [128, 128, 128], P('grid'), may hold values from -3 to 3
- external: float32 [128, 128, 128], P('grid'), may hold values from -6 to 6
- core_density: float32 [128, 128, 128], P('grid'), may hold values from 0.05 to 0.5
- rotations: float32 [2, 4, 2], P(None, 'band'), may hold values from -2 to 3
- mlp_in: float32 [3, 32], replicated, may hold values from -4 to 4
- mlp_out: float32 [32], replicated, may hold values from -0.4 to 0.4
Outputs:
- new_coefficients: float32 [4, 2, 128, 128, 128], P('band', None, 'grid')
- new_potential: float32 [128, 128, 128], P('grid')
All inputs are finite; a program needn't handle non-finite values.
Results may differ from a plain program's by a relative error of at most 0.0003.
Values sent between devices are 32-bit elements; how exact they have to be, the bound alone decides.
A program may use at most 64 MiB of HBM per device.

v0:
```python
import math
import jax
import jax.numpy as jnp
from jax import lax
from jax.sharding import PartitionSpec as P

NX = 128
NY = 128
NZ = 128
ITERS = 2
step_size = 0.2
epsilon = 1e-06
spacing = 0.58
kinetic_scale = 0.5 * (2.0 * math.pi / spacing) ** 2
coulomb_scale = spacing * spacing / math.pi
gradient_scale = 2.0 * math.pi / spacing
reduced_scale = 2.0 * (3.0 * math.pi * math.pi) ** (1.0 / 3.0)
exchange_scale = (3.0 / math.pi) ** (1.0 / 3.0)


def frequencies(points, offset, length):
    places = offset + lax.iota(jnp.int32, length)
    return jnp.where(2 * places < points, places, places - points)


def without_nyquist(values, points):
    return jnp.where(2 * values == -points, 0, values)


def reciprocal_tables(offset, length):
    along_x = frequencies(NX, offset, length)
    along_y = frequencies(NY, 0, NY)
    raw_z = frequencies(NZ, 0, NZ)
    along_z = raw_z * (NX // NZ)
    squared = (
        along_x[:, None, None] * along_x[:, None, None]
        + along_y[None, :, None] * along_y[None, :, None]
        + along_z[None, None, :] * along_z[None, None, :]
    )
    cutoff = (16 * squared <= NX * NX).astype(jnp.float32)
    kinetic = kinetic_scale * squared.astype(jnp.float32) / (NX * NX)
    coulomb = jnp.where(
        squared > 0, coulomb_scale * (NX * NX) / jnp.maximum(squared, 1).astype(jnp.float32), 0.0
    )
    slope_x = gradient_scale * without_nyquist(along_x, NX).astype(jnp.float32) / NX
    slope_y = gradient_scale * without_nyquist(along_y, NY).astype(jnp.float32) / NX
    slope_z = gradient_scale * (without_nyquist(raw_z, NZ) * (NX // NZ)).astype(jnp.float32) / NX
    return (
        cutoff,
        kinetic,
        coulomb,
        slope_x[:, None, None],
        slope_y[None, :, None],
        slope_z[None, None, :],
    )


def dft_tables(points, direction):
    places = lax.iota(jnp.int32, points)
    phases = places[:, None] * places[None, :] % points
    angles = phases.astype(jnp.float32) * (2.0 * math.pi / points)
    return (jnp.cos(angles), direction * jnp.sin(angles))


def transform(perceptron_levels, tables, pattern):
    highest = lax.Precision.HIGHEST
    cosine_table, sine_table = tables
    real_part = perceptron_levels[:, 0]
    imag_part = perceptron_levels[:, 1]
    new_real = jnp.einsum(pattern, real_part, cosine_table, precision=highest) - jnp.einsum(
        pattern, imag_part, sine_table, precision=highest
    )
    new_imag = jnp.einsum(pattern, real_part, sine_table, precision=highest) + jnp.einsum(
        pattern, imag_part, cosine_table, precision=highest
    )
    return jnp.stack([new_real, new_imag], 1)


def toward_position_grid(spectral_amplitude, fourier_synthesis, orbital_holder):
    perceptron_levels = transform(spectral_amplitude, fourier_synthesis[2], "bxyz,zw->bxyw")
    perceptron_levels = transform(perceptron_levels, fourier_synthesis[1], "bxyz,yv->bxvz")
    perceptron_levels = orbital_holder(perceptron_levels)
    return transform(perceptron_levels, fourier_synthesis[0], "bxyz,xu->byuz")


def toward_spectral_amplitudes(position_grid_values, fourier_analysis, orbital_holder):
    perceptron_levels = transform(position_grid_values, fourier_analysis[0], "byxz,xu->buyz")
    perceptron_levels = orbital_holder(perceptron_levels)
    perceptron_levels = transform(perceptron_levels, fourier_analysis[1], "bxyz,yv->bxvz")
    perceptron_levels = transform(perceptron_levels, fourier_analysis[2], "bxyz,zw->bxyw")
    return perceptron_levels / (NX * NY * NZ)


def body(coefficients, potential, external, core_density, rotations, mlp_in, mlp_out):
    highest = lax.Precision.HIGHEST
    planes = coefficients.shape[2]
    offset = lax.axis_index("grid") * planes
    cutoff, kinetic, coulomb, slope_x, slope_y, slope_z = reciprocal_tables(offset, planes)
    fourier_synthesis = (dft_tables(NX, 1.0), dft_tables(NY, 1.0), dft_tables(NZ, 1.0))
    fourier_analysis = (dft_tables(NX, -1.0), dft_tables(NY, -1.0), dft_tables(NZ, -1.0))

    def outward(perceptron_levels):
        return lax.all_to_all(perceptron_levels, "grid", split_axis=3, concat_axis=2, tiled=True)

    def inward(perceptron_levels):
        return lax.all_to_all(perceptron_levels, "grid", split_axis=2, concat_axis=3, tiled=True)

    current = cutoff * coefficients
    for iteration in range(ITERS):
        applied = cutoff * (
            kinetic * current
            + toward_spectral_amplitudes(
                toward_position_grid(current, fourier_synthesis, outward) * potential,
                fourier_analysis,
                inward,
            )
        )
        rotation = rotations[iteration]
        intersection, energy = lax.psum(
            (
                jnp.sum(current * current, axis=(1, 2, 3, 4)),
                jnp.sum(current * applied, axis=(1, 2, 3, 4)),
            ),
            "grid",
        )
        factor = 1.0 + step_size * (energy / (intersection + epsilon))
        updated = factor[:, None, None, None, None] * current - step_size * applied
        updated = jnp.einsum("ij,jcxyz->icxyz", rotation, updated, precision=highest)
        length = lax.psum(jnp.sum(updated * updated, axis=(1, 2, 3, 4)), "grid")
        current = updated / jnp.sqrt(length + epsilon)[:, None, None, None, None]
    real_space = toward_position_grid(current, fourier_synthesis, outward)
    bands_all = coefficients.shape[0] * lax.axis_size("band")
    partial_value = 2.0 / bands_all * jnp.sum(real_space * real_space, axis=(0, 1))
    density = lax.psum(partial_value, "band") + core_density
    spectrum = toward_spectral_amplitudes(
        jnp.stack([density, jnp.zeros_like(density)])[None], fourier_analysis, inward
    )[0]
    spec_real = spectrum[0]
    spec_imag = spectrum[1]
    first_real = coulomb * spec_real - slope_x * spec_real
    first_imag = coulomb * spec_imag - slope_x * spec_imag
    second_real = -slope_y * spec_imag - slope_z * spec_real
    second_imag = slope_y * spec_real - slope_z * spec_imag
    fields = toward_position_grid(
        jnp.stack([jnp.stack([first_real, first_imag]), jnp.stack([second_real, second_imag])]),
        fourier_synthesis,
        outward,
    )
    hartree = fields[0, 0]
    change_x = fields[0, 1]
    change_y = fields[1, 0]
    change_z = fields[1, 1]
    cube_root = jnp.cbrt(density)
    gradient = jnp.sqrt(change_x * change_x + change_y * change_y + change_z * change_z)
    reduced = gradient / (reduced_scale * density * cube_root)
    bounded = reduced / (1.0 + reduced)
    hidden = jnp.tanh(
        mlp_in[0][:, None, None, None] * cube_root
        + mlp_in[1][:, None, None, None] * bounded
        + mlp_in[2][:, None, None, None]
    )
    enhance = 1.0 + jnp.einsum("k,kyxz->yxz", mlp_out, hidden, precision=highest)
    new_potential = external + hartree - exchange_scale * cube_root * enhance
    return (current, new_potential)


def solution(mesh):
    in_specs = (
        P("band", None, "grid", None, None),
        P("grid", None, None),
        P("grid", None, None),
        P("grid", None, None),
        P(None, "band", None),
        P(),
        P(),
    )
    out_specs = (P("band", None, "grid", None, None), P("grid", None, None))
    return jax.shard_map(body, mesh=mesh, in_specs=in_specs, out_specs=out_specs, check_vma=False)
```

profile of v0, /device:TPU:12, one launch (start us, length us, event | category | flops | bytes accessed | tf_op | source)
XLA Modules:
  0.0 682.6 jit_solution(3617643584464941430)
XLA Ops:
  7.5 1.9 copy_multiply_fusion
  18.2 1.3 fusion.39
  21.0 54.6 %all_to_all.126 = f32[2,2,8,128,128]{4,2,0,1,3:T(8,128)S(1)} all-to-all(f32[2,2,8,128,128]{4,2,0,1,3:T(8,128)S(1)} %copy.58), channel_id=1, replica_groups=mesh['band'=2,'grid'=16] {'grid'}, dimensions={3} | all-to-all | bytes 4194304 | tf_op jit(solution)/shard_map/all_to_all | solution.py:103
  78.4 1.3 fusion.36
  79.8 1.4 fusion.37
  84.0 1.3 fusion.34
  85.3 1.3 fusion.35
  86.8 2.5 copy.60
  89.4 16.6 %all-to-all-start.1 = ((f32[2,2,128,8,128]{4,3,0,1,2:T(8,128)}), f32[2,2,128,8,128]{4,3,0,1,2:T(8,128)S(1)}, u32[]{:S(2)}, u32[]{:S(2)}) async-start(f32[2,2,128,8,128]{4,3,0,1,2:T(8,128)} %copy.60), calls=%async_computation.1 | async-start | bytes 4194304 | tf_op jit(solution)/shard_map/all_to_all | solution.py:106
  106.2 46.5 %all-to-all-done.1 = f32[2,2,128,8,128]{4,3,0,1,2:T(8,128)S(1)} async-done(((f32[2,2,128,8,128]{4,3,0,1,2:T(8,128)}), f32[2,2,128,8,128]{4,3,0,1,2:T(8,128)S(1)}, u32[]{:S(2)}, u32[]{:S(2)}) %all-to-all-start.1) | async-done | bytes 2097184 | tf_op jit(solution)/shard_map/all_to_all | solution.py:106
  164.8 29.5 %all-reduce.2 = (f32[2]{0:T(128)S(1)}, f32[2]{0:T(128)S(1)}) all-reduce(f32[2]{0:T(128)S(1)} %get-tuple-element.9, f32[2]{0:T(128)S(1)} %get-tuple-element.8), channel_id=1, replica_groups=mesh['band'=2,'grid'=16] {'grid'}, use_global_device_ids=true, to_apply=%region_1.2 | all-reduce | flops 4 | bytes 32 | tf_op jit(solution)/shard_map/psum | solution.py:119
  194.3 2.3 multiply_subtract_fusion.1
  196.7 9.5 %multiply_reduce_fusion.3 = (f32[2]{0:T(128)S(1)}, f32[2,8,128,128,2]{3,4,2,1,0:T(2,128)S(1)}) fusion(f32[2,2,2]{2,1,0:T(2,128)S(1)} %copy-done.11, f32[2,2,8,128,128]{4,3,2,0,1:T(8,128)S(1)} %multiply_subtract_fusion.1), kind=kOutput, calls=%fused_computation.35 | convolution fusion | flops 13631486 | bytes 4195336 | tf_op jit(solution)/shard_map/ij,jcxyz->icxyz/dot_general | solution.py:128
  206.1 37.0 %psum.51 = f32[2]{0:T(128)S(1)} all-reduce(f32[2]{0:T(128)S(1)} %get-tuple-element.27), channel_id=1, replica_groups=mesh['band'=2,'grid'=16] {'grid'}, use_global_device_ids=true, to_apply=%region_5.6 | all-reduce | flops 2 | bytes 16 | tf_op jit(solution)/shard_map/psum | solution.py:129
  251.0 1.3 fusion.28
  252.3 1.3 fusion.29
  255.1 44.4 %all_to_all.127 = f32[2,2,8,128,128]{4,2,0,1,3:T(8,128)S(1)} all-to-all(f32[2,2,8,128,128]{4,2,0,1,3:T(8,128)S(1)} %copy.72), channel_id=1, replica_groups=mesh['band'=2,'grid'=16] {'grid'}, dimensions={3} | all-to-all | bytes 4194304 | tf_op jit(solution)/shard_map/all_to_all | solution.py:103
  302.4 1.3 fusion.26
  303.7 1.4 fusion.27
  307.9 1.3 fusion.24
  309.3 1.3 fusion.25
  312.0 45.8 %all_to_all.128 = f32[2,2,128,8,128]{4,3,0,1,2:T(8,128)S(1)} all-to-all(f32[2,2,128,8,128]{4,3,0,1,2:T(8,128)S(1)} %copy.74), channel_id=1, replica_groups=mesh['band'=2,'grid'=16] {'grid'}, dimensions={2} | all-to-all | bytes 4194304 | tf_op jit(solution)/shard_map/all_to_all | solution.py:106
  369.3 29.9 %all-reduce.1 = (f32[2]{0:T(128)S(1)}, f32[2]{0:T(128)S(1)}) all-reduce(f32[2]{0:T(128)S(1)} %get-tuple-element.7, f32[2]{0:T(128)S(1)} %get-tuple-element.6), channel_id=1, replica_groups=mesh['band'=2,'grid'=16] {'grid'}, use_global_device_ids=true, to_apply=%region_7.8 | all-reduce | flops 4 | bytes 32 | tf_op jit(solution)/shard_map/psum | solution.py:119
  399.1 2.3 multiply_subtract_fusion
  401.4 9.9 %multiply_reduce_fusion = (f32[2]{0:T(128)S(1)}, f32[2,8,128,128,2]{3,4,2,1,0:T(2,128)}) fusion(f32[2,2,2]{2,1,0:T(2,128)S(1)} %copy-done.11, f32[2,2,8,128,128]{4,3,2,0,1:T(8,128)S(1)} %multiply_subtract_fusion), kind=kOutput, calls=%fused_computation.31 | convolution fusion | flops 13631486 | bytes 4195336 | tf_op jit(solution)/shard_map/ij,jcxyz->icxyz/dot_general | solution.py:128
  411.3 36.7 %psum.54 = f32[2]{0:T(128)S(1)} all-reduce(f32[2]{0:T(128)S(1)} %get-tuple-element.29), channel_id=1, replica_groups=mesh['band'=2,'grid'=16] {'grid'}, use_global_device_ids=true, to_apply=%region_11.12 | all-reduce | flops 2 | bytes 16 | tf_op jit(solution)/shard_map/psum | solution.py:129
  448.0 2.6 divide_bitcast_fusion
  458.3 1.3 fusion.19
  461.1 1.4 copy.89
  462.6 44.1 %all_to_all.129 = f32[2,2,8,128,128]{4,2,0,1,3:T(8,128)S(1)} all-to-all(f32[2,2,8,128,128]{4,2,0,1,3:T(8,128)S(1)} %copy.89), channel_id=1, replica_groups=mesh['band'=2,'grid'=16] {'grid'}, dimensions={3} | all-to-all | bytes 4194304 | tf_op jit(solution)/shard_map/all_to_all | solution.py:103
  509.5 1.3 fusion.16
  510.8 1.3 fusion.17
  513.2 18.1 %all-reduce.5.cloned.1.call-done = f32[8,128,128]{2,1,0:T(8,128)} async-done(((f32[8,128,128]{2,1,0:T(8,128)}), f32[8,128,128]{2,1,0:T(8,128)}) %all-reduce.5.cloned.1.call-update) | async-done | bytes 524304 | tf_op jit(solution)/shard_map/psum | solution.py:134
  531.3 2.3 fusion.639
  537.2 1.6 copy.91
  538.7 7.3 %all-to-all-start.5 = ((f32[1,2,128,8,128]{4,3,1,0,2:T(8,128)}), f32[1,2,128,8,128]{4,3,1,0,2:T(8,128)}, u32[]{:S(2)}, u32[]{:S(2)}) async-start(f32[1,2,128,8,128]{4,3,1,0,2:T(8,128)} %copy.91), calls=%async_computation.5 | async-start | bytes 2097152 | tf_op jit(solution)/shard_map/all_to_all | solution.py:106
  546.1 25.3 %all-to-all-done.5 = f32[1,2,128,8,128]{4,3,1,0,2:T(8,128)} async-done(((f32[1,2,128,8,128]{4,3,1,0,2:T(8,128)}), f32[1,2,128,8,128]{4,3,1,0,2:T(8,128)}, u32[]{:S(2)}, u32[]{:S(2)}) %all-to-all-start.5) | async-done | bytes 1048608 | tf_op jit(solution)/shard_map/all_to_all | solution.py:106
  571.4 1.3 copy.211
  584.0 1.5 fusion.137
  588.0 1.3 fusion.15
  590.8 2.5 copy.101
  593.3 5.9 all-to-all-start.6
  599.3 1.6 copy.103
  600.9 45.7 %all-to-all-done.6 = f32[2,2,8,128,128]{4,2,0,1,3:T(8,128)} async-done(((f32[2,2,8,128,128]{4,2,0,1,3:T(8,128)}), f32[2,2,8,128,128]{4,2,0,1,3:T(8,128)}, u32[]{:S(2)}, u32[]{:S(2)}) %all-to-all-start.6) | async-done | bytes 2097184 | tf_op jit(solution)/shard_map/all_to_all | solution.py:103
  646.6 1.8 copy.205
  652.3 1.4 fusion.13
  654.4 4.3 add_tanh_fusion
  658.8 15.2 %fusion = f32[1,8,128,128]{3,0,2,1:T(1,128)S(1)} fusion(f32[32,8,128,128]{3,2,1,0:T(8,128)S(1)} %add_tanh_fusion, f32[32]{0:T(128)S(1)} %copy-done), kind=kOutput, calls=%fused_computation | convolution fusion | flops 50331648 | bytes 17301632 | tf_op jit(solution)/shard_map/k,kyxz->yxz/dot_general | solution.py:162
  (135 shorter events, 93.9 us)
Async XLA Ops:
  7.2 651.6 %copy-start = (f32[32]{0:T(128)S(1)}, f32[32]{0:T(128)}, u32[]{:S(2)}) copy-start(f32[32]{0:T(128)} %param.13) | copy-start | bytes 388
  79.8 1.4 copy-start.6
  89.4 63.3 %all-to-all-start.1 = ((f32[2,2,128,8,128]{4,3,0,1,2:T(8,128)}), f32[2,2,128,8,128]{4,3,0,1,2:T(8,128)S(1)}, u32[]{:S(2)}, u32[]{:S(2)}) async-start(f32[2,2,128,8,128]{4,3,0,1,2:T(8,128)} %copy.60), calls=%async_computation.1 | async-start | bytes 4194304 | tf_op jit(solution)/shard_map/all_to_all | solution.py:106
  106.0 425.3 %all-reduce.5.cloned.1.call-start = ((), (), s32[]{:S(2)}) async-start(), calls=%async_computation.7 | async-start | bytes 1048576 | tf_op jit(solution)/shard_map/psum | solution.py:134
  161.9 2.9 copy-start.4
  161.9 2.0 copy-start.1
  163.9 1.0 copy-start.5
  194.3 2.3 copy-start.11
  303.7 1.4 copy-start.7
  366.9 2.3 copy-start.2
  368.2 1.1 copy-start.3
  512.1 19.1 %copy-start.9 = (f32[8,128,128]{2,1,0:T(8,128)S(1)}, f32[8,128,128]{2,1,0:T(8,128)}, u32[]{:S(2)}) copy-start(f32[8,128,128]{2,1,0:T(8,128)} %param.10) | copy-start | bytes 1572868
  538.7 32.7 %all-to-all-start.5 = ((f32[1,2,128,8,128]{4,3,1,0,2:T(8,128)}), f32[1,2,128,8,128]{4,3,1,0,2:T(8,128)}, u32[]{:S(2)}, u32[]{:S(2)}) async-start(f32[1,2,128,8,128]{4,3,1,0,2:T(8,128)} %copy.91), calls=%async_computation.5 | async-start | bytes 2097152 | tf_op jit(solution)/shard_map/all_to_all | solution.py:106
  593.3 6.0 copy-start.10
  593.3 53.2 %all-to-all-start.6 = ((f32[2,2,8,128,128]{4,2,0,1,3:T(8,128)}), f32[2,2,8,128,128]{4,2,0,1,3:T(8,128)}, u32[]{:S(2)}, u32[]{:S(2)}) async-start(f32[2,2,8,128,128]{4,2,0,1,3:T(8,128)} %copy.101), calls=%async_computation.6 | async-start | bytes 4194304 | tf_op jit(solution)/shard_map/all_to_all | solution.py:103
  658.8 15.3 %copy-start.8 = (f32[8,128,128]{2,1,0:T(8,128)S(1)}, f32[8,128,128]{2,1,0:T(8,128)}, u32[]{:S(2)}) copy-start(f32[8,128,128]{2,1,0:T(8,128)} %param.9) | copy-start | bytes 1572868
Sparse Core Ops, SparseCore 0:
  513.3 17.9 all-reduce.4
where the time goes:
time: 692 us; the launch traced here: 683 us
  blocking collectives  322 us (47%)
  matrix products  137 us (20%)
  waiting for transfers between devices  136 us (20%)
  starting transfers between devices  29.9 us (4%)
  other arithmetic  24 us (3%)
  local copies, waits for them, and re-layouts  18.7 us (3%)
  between operations  15.6 us (2%)
    all_to_all x3, blocking collectives, outward(): lax.all_to_all(perceptron_levels, 'grid', split_axis=3, concat_axis=2, ti...  143 us
    psum x2, blocking collectives, body(): length = lax.psum(jnp.sum(updated * updated, axis=(1, 2, 3, 4)), 'grid')  73.7 us
    all_to_all x2, waiting for transfers between devices, inward(): lax.all_to_all(perceptron_levels, 'grid', split_axis=2, concat_axis=3, ti...  71.8 us
    psum x2, blocking collectives, body(): lax.psum((jnp.sum(current * current, axis=(1, 2, 3, 4)), jnp.sum(current...  59.3 us
    all_to_all x1, blocking collectives, inward(): lax.all_to_all(perceptron_levels, 'grid', split_axis=2, concat_axis=3, ti...  45.8 us
    all_to_all x1, waiting for transfers between devices, outward(): lax.all_to_all(perceptron_levels, 'grid', split_axis=3, concat_axis=2, ti...  45.7 us
    dot_general x21, matrix products, transform(): jnp.einsum(pattern, imag_part, sine_table, precision=highest)  25.9 us
    dot_general x21, matrix products, transform(): jnp.einsum(pattern, imag_part, cosine_table, precision=highest)  25.7 us
  transfers between devices with their start and end apart: 4, of which 4 were waited for; matrix products, arithmetic and copies ran while one was open for 0% of the time, Pallas kernels for 0%

commit v1 on v0

--- a/solution.py
+++ b/solution.py
@@ -100,7 +100,12 @@
     fourier_analysis = (dft_tables(NX, -1.0), dft_tables(NY, -1.0), dft_tables(NZ, -1.0))
 
     def outward(perceptron_levels):
-        return lax.all_to_all(perceptron_levels, "grid", split_axis=3, concat_axis=2, tiled=True)
+        return jnp.concatenate(
+            lax.all_to_all(
+                jnp.stack(jnp.split(perceptron_levels, lax.axis_size("grid"), axis=3)), "grid", 0, 0
+            ),
+            axis=2,
+        )
 
     def inward(perceptron_levels):
         return lax.all_to_all(perceptron_levels, "grid", split_axis=2, concat_axis=3, tiled=True)

time: 692 us -> 687 us (level)
  starting transfers between devices: 29.9 us -> 18.5 us
  other arithmetic: 24 us -> 34.8 us
    all_to_all x2, starting transfers between devices: 23.9 us -> 12.8 us  [inward(): lax.all_to_all(perceptron_levels, 'grid', split_axis=2, concat_axis=3, ti...]
    unnamed x0 -> x60, other arithmetic: none -> 10.9 us
where the time goes in v1:
time: 687 us; the launch traced here: 678 us
  blocking collectives  323 us (47%)
  matrix products  137 us (20%)
  waiting for transfers between devices  137 us (20%)
  other arithmetic  34.8 us (5%)
  starting transfers between devices  18.5 us (3%)
  between operations  15.7 us (2%)
  local copies, waits for them, and re-layouts  12.8 us (2%)
    all_to_all x3, blocking collectives, outward(): lax.all_to_all(jnp.stack(jnp.split(perceptron_levels, lax.axis_size('grid...  144 us
    psum x2, blocking collectives, body(): length = lax.psum(jnp.sum(updated * updated, axis=(1, 2, 3, 4)), 'grid')  73.1 us
    all_to_all x2, waiting for transfers between devices, inward(): lax.all_to_all(perceptron_levels, 'grid', split_axis=2, concat_axis=3, ti...  72.7 us
    psum x2, blocking collectives, body(): lax.psum((jnp.sum(current * current, axis=(1, 2, 3, 4)), jnp.sum(current...  59.4 us
    all_to_all x1, blocking collectives, inward(): lax.all_to_all(perceptron_levels, 'grid', split_axis=2, concat_axis=3, ti...  46 us
    all_to_all x1, waiting for transfers between devices, outward(): lax.all_to_all(jnp.stack(jnp.split(perceptron_levels, lax.axis_size('grid...  45.9 us
    dot_general x21, matrix products, transform(): jnp.einsum(pattern, imag_part, sine_table, precision=highest)  25.8 us
    dot_general x21, matrix products, transform(): jnp.einsum(pattern, imag_part, cosine_table, precision=highest)  25.7 us
  transfers between devices with their start and end apart: 4, of which 4 were waited for; matrix products, arithmetic and copies ran while one was open for 0% of the time, Pallas kernels for 0%

profile of v1, /device:TPU:12, one launch (start us, length us, event | category | flops | bytes accessed | tf_op | source)
XLA Modules:
  0.0 678.4 jit_solution(9342625213865868539)
XLA Ops:
  7.5 1.9 copy_multiply_fusion
  19.9 54.8 %all_to_all.74 = f32[16,2,2,8,8,128]{5,4,3,1,2,0:T(8,128)S(1)} all-to-all(f32[16,2,2,8,8,128]{5,4,3,1,2,0:T(8,128)S(1)} %constant_dynamic-update-slice_fusion), channel_id=1, replica_groups=mesh['band'=2,'grid'=16] {'grid'}, dimensions={0} | all-to-all | bytes 4194304 | tf_op jit(solution)/shard_map/all_to_all | solution.py:104
  76.4 1.3 fusion.50
  77.7 1.4 fusion.37
  79.1 1.4 fusion.36
  83.4 1.3 fusion.34
  84.7 1.3 fusion.35
  86.2 2.5 copy.109
  88.7 5.5 all-to-all-start.1
  94.5 47.4 %all-to-all-done.1 = f32[2,2,128,8,128]{4,3,0,1,2:T(8,128)S(1)} async-done(((f32[2,2,128,8,128]{4,3,0,1,2:T(8,128)}), f32[2,2,128,8,128]{4,3,0,1,2:T(8,128)S(1)}, u32[]{:S(2)}, u32[]{:S(2)}) %all-to-all-start.1) | async-done | bytes 2097184 | tf_op jit(solution)/shard_map/all_to_all | solution.py:111
  142.2 1.3 fusion.61
  154.0 29.7 %all-reduce.2 = (f32[2]{0:T(128)S(1)}, f32[2]{0:T(128)S(1)}) all-reduce(f32[2]{0:T(128)S(1)} %get-tuple-element.11, f32[2]{0:T(128)S(1)} %get-tuple-element.10), channel_id=1, replica_groups=mesh['band'=2,'grid'=16] {'grid'}, use_global_device_ids=true, to_apply=%region_1.2 | all-reduce | flops 4 | bytes 32 | tf_op jit(solution)/shard_map/psum | solution.py:124
  183.8 2.3 multiply_subtract_fusion.1
  186.1 9.5 %multiply_reduce_fusion.3 = (f32[2]{0:T(128)S(1)}, f32[2,8,128,128,2]{3,4,2,1,0:T(2,128)S(1)}) fusion(f32[2,2,2]{2,1,0:T(2,128)S(1)} %copy-done.11, f32[2,2,8,128,128]{4,3,2,0,1:T(8,128)S(1)} %multiply_subtract_fusion.1), kind=kOutput, calls=%fused_computation.147 | convolution fusion | flops 13631486 | bytes 4195336 | tf_op jit(solution)/shard_map/ij,jcxyz->icxyz/dot_general | solution.py:133
  195.5 36.2 %psum.51 = f32[2]{0:T(128)S(1)} all-reduce(f32[2]{0:T(128)S(1)} %get-tuple-element.37), channel_id=1, replica_groups=mesh['band'=2,'grid'=16] {'grid'}, use_global_device_ids=true, to_apply=%region_5.6 | all-reduce | flops 2 | bytes 16 | tf_op jit(solution)/shard_map/psum | solution.py:134
  242.7 45.2 %all_to_all.75 = f32[16,2,2,8,8,128]{5,4,3,1,2,0:T(8,128)S(1)} all-to-all(f32[16,2,2,8,8,128]{5,4,3,1,2,0:T(8,128)S(1)} %constant_dynamic-update-slice_fusion.16), channel_id=1, replica_groups=mesh['band'=2,'grid'=16] {'grid'}, dimensions={0} | all-to-all | bytes 4194304 | tf_op jit(solution)/shard_map/all_to_all | solution.py:104
  289.5 1.3 fusion.52
  290.8 1.4 fusion.27
  292.2 1.4 fusion.26
  296.5 1.3 fusion.24
  297.8 1.3 fusion.25
  300.5 46.0 %all_to_all.76 = f32[2,2,128,8,128]{4,3,0,1,2:T(8,128)S(1)} all-to-all(f32[2,2,128,8,128]{4,3,0,1,2:T(8,128)S(1)} %copy.124), channel_id=1, replica_groups=mesh['band'=2,'grid'=16] {'grid'}, dimensions={2} | all-to-all | bytes 4194304 | tf_op jit(solution)/shard_map/all_to_all | solution.py:111
  353.1 1.3 fusion.22
  358.0 29.7 %all-reduce.1 = (f32[2]{0:T(128)S(1)}, f32[2]{0:T(128)S(1)}) all-reduce(f32[2]{0:T(128)S(1)} %get-tuple-element.9, f32[2]{0:T(128)S(1)} %get-tuple-element.8), channel_id=1, replica_groups=mesh['band'=2,'grid'=16] {'grid'}, use_global_device_ids=true, to_apply=%region_7.8 | all-reduce | flops 4 | bytes 32 | tf_op jit(solution)/shard_map/psum | solution.py:124
  387.8 2.3 multiply_subtract_fusion
  390.0 9.9 %multiply_reduce_fusion = (f32[2]{0:T(128)S(1)}, f32[2,8,128,128,2]{3,4,2,1,0:T(2,128)}) fusion(f32[2,2,2]{2,1,0:T(2,128)S(1)} %copy-done.11, f32[2,2,8,128,128]{4,3,2,0,1:T(8,128)S(1)} %multiply_subtract_fusion), kind=kOutput, calls=%fused_computation.143 | convolution fusion | flops 13631486 | bytes 4195336 | tf_op jit(solution)/shard_map/ij,jcxyz->icxyz/dot_general | solution.py:133
  399.9 37.0 %psum.54 = f32[2]{0:T(128)S(1)} all-reduce(f32[2]{0:T(128)S(1)} %get-tuple-element.39), channel_id=1, replica_groups=mesh['band'=2,'grid'=16] {'grid'}, use_global_device_ids=true, to_apply=%region_11.12 | all-reduce | flops 2 | bytes 16 | tf_op jit(solution)/shard_map/psum | solution.py:134
  436.9 2.6 divide_bitcast_fusion
  450.2 44.5 %all_to_all.77 = f32[16,2,2,8,8,128]{5,4,3,1,2,0:T(8,128)S(1)} all-to-all(f32[16,2,2,8,8,128]{5,4,3,1,2,0:T(8,128)S(1)} %constant_dynamic-update-slice_fusion.32), channel_id=1, replica_groups=mesh['band'=2,'grid'=16] {'grid'}, dimensions={0} | all-to-all | bytes 4194304 | tf_op jit(solution)/shard_map/all_to_all | solution.py:104
  496.3 1.3 fusion.54
  497.7 1.3 fusion.17
  499.0 1.3 fusion.16
  501.4 18.1 %all-reduce.5.cloned.1.call-done = f32[8,128,128]{2,1,0:T(8,128)} async-done(((f32[8,128,128]{2,1,0:T(8,128)}), f32[8,128,128]{2,1,0:T(8,128)}) %all-reduce.5.cloned.1.call-update) | async-done | bytes 524304 | tf_op jit(solution)/shard_map/psum | solution.py:139
  519.4 2.3 fusion.703
  525.3 1.6 copy.142
  526.9 7.3 %all-to-all-start.5 = ((f32[1,2,128,8,128]{4,3,1,0,2:T(8,128)}), f32[1,2,128,8,128]{4,3,1,0,2:T(8,128)}, u32[]{:S(2)}, u32[]{:S(2)}) async-start(f32[1,2,128,8,128]{4,3,1,0,2:T(8,128)} %copy.142), calls=%async_computation.5 | async-start | bytes 2097152 | tf_op jit(solution)/shard_map/all_to_all | solution.py:111
  534.3 25.3 %all-to-all-done.5 = f32[1,2,128,8,128]{4,3,1,0,2:T(8,128)} async-done(((f32[1,2,128,8,128]{4,3,1,0,2:T(8,128)}), f32[1,2,128,8,128]{4,3,1,0,2:T(8,128)}, u32[]{:S(2)}, u32[]{:S(2)}) %all-to-all-start.5) | async-done | bytes 1048608 | tf_op jit(solution)/shard_map/all_to_all | solution.py:111
  559.6 1.3 copy.287
  572.1 1.5 fusion.201
  589.4 5.6 all-to-all-start.6
  595.1 1.6 copy.155
  596.7 45.9 %all-to-all-done.6 = f32[16,2,2,8,8,128]{5,4,3,1,2,0:T(8,128)} async-done(((f32[16,2,2,8,8,128]{5,4,3,1,2,0:T(8,128)}), f32[16,2,2,8,8,128]{5,4,3,1,2,0:T(8,128)}, u32[]{:S(2)}, u32[]{:S(2)}) %all-to-all-start.6) | async-done | bytes 2097184 | tf_op jit(solution)/shard_map/all_to_all | solution.py:104
  642.5 1.7 copy.152
  645.7 1.3 fusion.56
  647.0 1.4 fusion.13
  648.4 1.3 fusion.12
  650.5 4.3 add_tanh_fusion
  654.9 15.2 %fusion = f32[1,8,128,128]{3,0,2,1:T(1,128)S(1)} fusion(f32[32,8,128,128]{3,2,1,0:T(8,128)S(1)} %add_tanh_fusion, f32[32]{0:T(128)S(1)} %copy-done), kind=kOutput, calls=%fused_computation | convolution fusion | flops 50331648 | bytes 17301632 | tf_op jit(solution)/shard_map/k,kyxz->yxz/dot_general | solution.py:167
  (195 shorter events, 100.2 us)
Async XLA Ops:
  7.2 647.7 %copy-start = (f32[32]{0:T(128)S(1)}, f32[32]{0:T(128)}, u32[]{:S(2)}) copy-start(f32[32]{0:T(128)} %param.13) | copy-start | bytes 388
  79.1 1.4 copy-start.6
  88.7 53.2 %all-to-all-start.1 = ((f32[2,2,128,8,128]{4,3,0,1,2:T(8,128)}), f32[2,2,128,8,128]{4,3,0,1,2:T(8,128)S(1)}, u32[]{:S(2)}, u32[]{:S(2)}) async-start(f32[2,2,128,8,128]{4,3,0,1,2:T(8,128)} %copy.109), calls=%async_computation.1 | async-start | bytes 4194304 | tf_op jit(solution)/shard_map/all_to_all | solution.py:111
  94.2 425.2 %all-reduce.5.cloned.1.call-start = ((), (), s32[]{:S(2)}) async-start(), calls=%async_computation.7 | async-start | bytes 1048576 | tf_op jit(solution)/shard_map/psum | solution.py:139
  151.0 2.9 copy-start.4
  151.1 2.0 copy-start.1
  153.0 1.0 copy-start.5
  183.8 2.3 copy-start.11
  292.2 1.4 copy-start.7
  355.7 2.3 copy-start.2
  357.0 1.1 copy-start.3
  500.3 19.1 %copy-start.9 = (f32[8,128,128]{2,1,0:T(8,128)S(1)}, f32[8,128,128]{2,1,0:T(8,128)}, u32[]{:S(2)}) copy-start(f32[8,128,128]{2,1,0:T(8,128)} %param.10) | copy-start | bytes 1572868
  526.9 32.7 %all-to-all-start.5 = ((f32[1,2,128,8,128]{4,3,1,0,2:T(8,128)}), f32[1,2,128,8,128]{4,3,1,0,2:T(8,128)}, u32[]{:S(2)}, u32[]{:S(2)}) async-start(f32[1,2,128,8,128]{4,3,1,0,2:T(8,128)} %copy.142), calls=%async_computation.5 | async-start | bytes 2097152 | tf_op jit(solution)/shard_map/all_to_all | solution.py:111
  589.4 5.6 copy-start.10
  589.4 53.1 %all-to-all-start.6 = ((f32[16,2,2,8,8,128]{5,4,3,1,2,0:T(8,128)}), f32[16,2,2,8,8,128]{5,4,3,1,2,0:T(8,128)}, u32[]{:S(2)}, u32[]{:S(2)}) async-start(f32[16,2,2,8,8,128]{5,4,3,1,2,0:T(8,128)} %constant_dynamic-update-slice_fusion.48), calls=%async_computation.6 | async-start | bytes 4194304 | tf_op jit(solution)/shard_map/all_to_all | solution.py:104
  654.8 15.2 %copy-start.8 = (f32[8,128,128]{2,1,0:T(8,128)S(1)}, f32[8,128,128]{2,1,0:T(8,128)}, u32[]{:S(2)}) copy-start(f32[8,128,128]{2,1,0:T(8,128)} %param.9) | copy-start | bytes 1572868
Sparse Core Ops, SparseCore 0:
  501.5 17.8 all-reduce.4
